TPU v7x, 256 devices: a whole 4x4x8 slice. The times are simulated.
256 devices in a mesh: row: 8 (over y, core), col: 32 (over x, z).
Axes of the slice: x: 4, y: 4, z: 8, core: 2. Of those that a mesh axis runs over, the one named last changes fastest.
Arguments:
- tokens: bfloat16 [2048, 6144], P('row', 'col'), may hold values from -6 to 6
- cotangent: bfloat16 [2048, 6144], P('row', 'col'), may hold values from -6 to 6
- w_expand: bfloat16 [6144, 12288], P('row', 'col'), may hold values from -0.078125 to 0.078125
- w_reduce: bfloat16 [6144, 12288], P('row', 'col'), may hold values from -0.0546875 to 0.0546875
- expand_mean: bfloat16 [6144, 12288], P('row', 'col'), may hold values from -1 to 1
- expand_mean_scale: float32 [24, 12288], P('row', 'col'), may hold values from 4 to 16
- expand_var: bfloat16 [6144, 12288], P('row', 'col'), may hold values from 0.049804688 to 1
- expand_var_scale: float32 [24, 12288], P('row', 'col'), may hold values from 4 to 16
- reduce_mean: bfloat16 [6144, 12288], P('row', 'col'), may hold values from -1 to 1
- reduce_mean_scale: float32 [24, 12288], P('row', 'col'), may hold values from 4 to 16
- reduce_var: bfloat16 [6144, 12288], P('row', 'col'), may hold values from 0.049804688 to 1
- reduce_var_scale: float32 [24, 12288], P('row', 'col'), may hold values from 4 to 16
Outputs:
- grad_tokens: bfloat16 [2048, 6144], P('row', 'col')
- new_expand: bfloat16 [6144, 12288], P('row', 'col')
- expand_mean_next: bfloat16 [6144, 12288], P('row', 'col')
- expand_mean_scale_next: float32 [24, 12288], P('row', 'col')
- expand_var_next: bfloat16 [6144, 12288], P('row', 'col')
- expand_var_scale_next: float32 [24, 12288], P('row', 'col')
- new_reduce: bfloat16 [6144, 12288], P('row', 'col')
- reduce_mean_next: bfloat16 [6144, 12288], P('row', 'col')
- reduce_mean_scale_next: float32 [24, 12288], P('row', 'col')
- reduce_var_next: bfloat16 [6144, 12288], P('row', 'col')
- reduce_var_scale_next: float32 [24, 12288], P('row', 'col')
All inputs are finite; a program needn't handle non-finite values.
Results may differ from a plain program's by a relative error of at most 0.0049.
Values may be sent and summed in bfloat16 or wider, within the bound.
No kernel may reach another device: no remote copies, remote signals or barrier semaphores. Data moves between devices by JAX's collectives and lax.ppermute only.
A program may use at most 128 MiB of HBM per device.

v0:
```python
import jax
import jax.numpy as jnp
from jax import lax
from jax.sharding import PartitionSpec as P

STEP = 10
beta_one = 0.9
beta_two = 0.999
adam_eps = 1e-08
learn_rate = 0.001
decay_rate = 0.1
scale_eps = 1e-06


def gelu_pair(pre_act):
    cdf_part = 0.5 * (1.0 + lax.erf(pre_act * 0.7071067811865476))
    slope = cdf_part + pre_act * jnp.exp(-0.5 * pre_act * pre_act) * 0.3989422804014327
    return (pre_act * cdf_part, slope)


def spread_scale(values, scale):
    blocks = scale.shape[0]
    shaped = values.reshape(blocks, values.shape[0] // blocks, values.shape[1])
    return (shaped * scale[:, None, :]).reshape(values.shape)


def block_max(values, blocks):
    shaped = values.reshape(blocks, values.shape[0] // blocks, values.shape[1])
    return jnp.max(jnp.abs(shaped), axis=1) + scale_eps


def adam_step(weight, grad_w, mean_q, mean_scale, var_q, var_scale):
    blocks = mean_scale.shape[0]
    mean_new = (
        beta_one * spread_scale(mean_q.astype(jnp.float32), mean_scale) + (1.0 - beta_one) * grad_w
    )
    var_new = (
        beta_two * spread_scale(var_q.astype(jnp.float32), var_scale)
        + (1.0 - beta_two) * grad_w * grad_w
    )
    mean_hat = mean_new / (1.0 - beta_one**STEP)
    var_hat = var_new / (1.0 - beta_two**STEP)
    old_weight = weight.astype(jnp.float32)
    new_weight = (
        old_weight
        - learn_rate * (mean_hat / (jnp.sqrt(var_hat) + adam_eps) + decay_rate * old_weight)
    ).astype(jnp.bfloat16)
    mean_scale_next = block_max(mean_new, blocks)
    var_scale_next = block_max(var_new, blocks)
    mean_next = spread_scale(mean_new, 1.0 / mean_scale_next).astype(jnp.bfloat16)
    var_next = spread_scale(var_new, 1.0 / var_scale_next).astype(jnp.bfloat16)
    return (new_weight, mean_next, mean_scale_next, var_next, var_scale_next)


def contract_first(left, right):
    return lax.dot_general(
        left, right, (((0,), (0,)), ((), ())), preferred_element_type=jnp.float32
    )


def local(
    tokens,
    cotangent,
    w_expand,
    w_reduce,
    expand_mean,
    expand_mean_scale,
    expand_var,
    expand_var_scale,
    reduce_mean,
    reduce_mean_scale,
    reduce_var,
    reduce_var_scale,
):
    token_rows, cot_rows = (
        lax.all_gather(tokens, "col", axis=1, tiled=True),
        lax.all_gather(cotangent, "col", axis=1, tiled=True),
    )
    input_whole, cot_whole = (
        lax.all_to_all(token_rows, "row", split_axis=1, concat_axis=0, tiled=True),
        lax.all_to_all(cot_rows, "row", split_axis=1, concat_axis=0, tiled=True),
    )
    up_panel, down_panel = (
        lax.all_gather(w_expand, "row", axis=0, tiled=True),
        lax.all_gather(w_reduce, "row", axis=0, tiled=True),
    )
    pre_act = jnp.dot(token_rows, up_panel, preferred_element_type=jnp.float32)
    act_grad = jnp.dot(cot_rows, down_panel, preferred_element_type=jnp.float32)
    activated, slope = gelu_pair(pre_act)
    activated = activated.astype(jnp.bfloat16)
    pre_grad = (act_grad * slope).astype(jnp.bfloat16)
    grad_cols = lax.psum_scatter(
        lax.dot_general(
            up_panel, pre_grad, (((1,), (1,)), ((), ())), preferred_element_type=jnp.float32
        ),
        "col",
        scatter_dimension=0,
        tiled=True,
    )
    grad_tokens = grad_cols.T.astype(jnp.bfloat16)
    grad_expand = contract_first(input_whole, lax.all_gather(pre_grad, "row", axis=0, tiled=True))
    grad_reduce = contract_first(cot_whole, lax.all_gather(activated, "row", axis=0, tiled=True))
    first = adam_step(
        w_expand, grad_expand, expand_mean, expand_mean_scale, expand_var, expand_var_scale
    )
    second = adam_step(
        w_reduce, grad_reduce, reduce_mean, reduce_mean_scale, reduce_var, reduce_var_scale
    )
    return (
        grad_tokens,
        first[0],
        first[1],
        first[2],
        first[3],
        first[4],
        second[0],
        second[1],
        second[2],
        second[3],
        second[4],
    )


def solution(mesh):
    placed = (
        P("row", "col"),
        P("row", "col"),
        P("row", "col"),
        P("row", "col"),
        P("row", "col"),
        P("row", "col"),
        P("row", "col"),
        P("row", "col"),
        P("row", "col"),
        P("row", "col"),
        P("row", "col"),
        P("row", "col"),
    )
    return jax.shard_map(
        local,
        mesh=mesh,
        in_specs=placed,
        out_specs=(
            P("row", "col"),
            P("row", "col"),
            P("row", "col"),
            P("row", "col"),
            P("row", "col"),
            P("row", "col"),
            P("row", "col"),
            P("row", "col"),
            P("row", "col"),
            P("row", "col"),
            P("row", "col"),
        ),
        check_vma=False,
    )
```

profile of v0, /device:TPU:8, one launch (start us, length us, event | category | flops | bytes accessed | tf_op | source)
XLA Modules:
  0.0 555.6 jit_solution(1710327823756502407)
XLA Ops:
  10.0 82.9 %all-gather.11.cloned.1.call-done = bf16[256,6144]{0,1:T(8,128)(2,1)} async-done(((bf16[256,192]{0,1:T(8,128)(2,1)}), bf16[256,6144]{0,1:T(8,128)(2,1)}) %all-gather.11.cloned.1.call-update) | async-done | bytes 3145744 | tf_op jit(solution)/shard_map/all_gather | solution.py:76
  92.9 34.3 %all-gather.13.cloned.1.call-done = bf16[6144,384]{1,0:T(8,128)(2,1)} async-done(((bf16[768,384]{1,0:T(8,128)(2,1)}), bf16[6144,384]{1,0:T(8,128)(2,1)}) %all-gather.13.cloned.1.call-update) | async-done | bytes 4718608 | tf_op jit(solution)/shard_map/all_gather | solution.py:84
  127.2 5.8 %multiply_convert_fusion.4 = (bf16[256,384]{1,0:T(8,128)(2,1)}, f32[256,384]{1,0:T(8,128)S(1)}) fusion(bf16[256,6144]{0,1:T(8,128)(2,1)} %all-gather.11.cloned.1.call-done, bf16[6144,384]{1,0:T(8,128)(2,1)} %all-gather.13.cloned.1.call-done), kind=kOutput, calls=%fused_computation.30 | convolution fusion | flops 1208451072 | bytes 8454144 | tf_op jit(solution)/shard_map/dot_general | solution.py:87
  133.1 77.2 %all-gather.7.cloned.1.call-done = bf16[256,6144]{0,1:T(8,128)(2,1)} async-done(((bf16[256,192]{0,1:T(8,128)(2,1)}), bf16[256,6144]{0,1:T(8,128)(2,1)}) %all-gather.7.cloned.1.call-update) | async-done | bytes 3145744 | tf_op jit(solution)/shard_map/all_gather | solution.py:77
  210.2 34.2 %all-gather.9.cloned.1.call-done = bf16[6144,384]{1,0:T(8,128)(2,1)} async-done(((bf16[768,384]{1,0:T(8,128)(2,1)}), bf16[6144,384]{1,0:T(8,128)(2,1)}) %all-gather.9.cloned.1.call-update) | async-done | bytes 4718608 | tf_op jit(solution)/shard_map/all_gather | solution.py:85
  244.4 5.9 %fusion.8 = bf16[256,384]{1,0:T(8,128)(2,1)} fusion(bf16[256,6144]{0,1:T(8,128)(2,1)} %all-gather.7.cloned.1.call-done, bf16[6144,384]{1,0:T(8,128)(2,1)} %all-gather.9.cloned.1.call-done, f32[256,384]{1,0:T(8,128)S(1)} %get-tuple-element.82), kind=kOutput, calls=%fused_computation.24 | convolution fusion | flops 1208942592 | bytes 8454144 | tf_op jit(solution)/shard_map/dot_general | solution.py:88
  250.9 7.0 %convolution_bitcast_fusion = f32[6144,256]{0,1:T(8,128)} fusion(bf16[256,384]{1,0:T(8,128)(2,1)} %fusion.8, bf16[6144,384]{1,0:T(8,128)(2,1)} %all-gather.13.cloned.1.call-done), kind=kOutput, calls=%fused_computation | convolution fusion | flops 1207959552 | bytes 11206656 | tf_op jit(solution)/shard_map/dot_general | solution.py:93
  257.9 6.6 %copy.123 = f32[6144,256]{1,0:T(8,128)} copy(f32[6144,256]{0,1:T(8,128)} %convolution_bitcast_fusion) | data formatting | bytes 12582912
  264.5 1.9 copy-done
  266.4 49.7 %all_to_all.38 = bf16[256,8,768]{0,2,1:T(8,128)(2,1)} all-to-all(bf16[256,8,768]{0,2,1:T(8,128)(2,1)S(1)} %bitcast.38), channel_id=1, replica_groups=mesh['row'=8,'col'=32] {'row'}, dimensions={1} | all-to-all | bytes 6291456 | tf_op jit(solution)/shard_map/all_to_all | solution.py:80
  316.1 4.0 all-to-all-start.1
  320.2 2.1 copy.96
  322.3 2.1 copy.106
  324.4 1.1 mul.182
  325.5 2.7 copy.101
  329.3 2.7 copy.98
  332.0 2.1 copy.100
  334.1 2.1 copy.97
  336.3 1.1 mul.196
  337.4 2.7 copy.108
  340.0 1.1 mul.202
  341.2 2.7 copy.111
  343.8 2.1 copy.107
  346.0 2.1 copy.110
  348.1 4.7 copy.99
  352.8 4.3 all-to-all-done.1
  357.1 2.9 copy.109
  360.0 6.3 %fusion.18 = (f32[768,384]{0,1:T(8,128)}, f32[768,384]{0,1:T(8,128)S(1)}, f32[768,384]{0,1:T(8,128)S(1)}, f32[768,384]{0,1:T(8,128)S(1)}) fusion(f32[768,384]{0,1:T(8,128)} %copy.98, bf16[768,384]{0,1:T(8,128)(2,1)} %copy.97, f32[768,384]{0,1:T(8,128)} %copy.101, bf16[768,384]{0,1:T(8,128)(2,1)} %copy.100, ...), kind=kOutput, calls=%fused_computation.44 | convolution fusion | flops 1211793408 | bytes 12976128 | tf_op jit(solution)/shard_map/dot_general | solution.py:56
  366.3 2.7 copy.102
  369.0 1.4 copy.104
  370.4 1.4 reduce_max.36
  372.7 1.3 broadcast_divide_fusion.2
  373.9 1.1 mul.190
  375.0 1.6 copy.103
  376.7 1.1 mul.193
  377.8 2.7 copy.105
  380.5 3.5 multiply_convert_fusion.2
  384.0 2.3 copy.117
  386.2 2.1 copy.118
  388.4 2.1 copy.119
  390.5 6.4 %fusion.15 = (f32[768,384]{0,1:T(8,128)}, f32[768,384]{0,1:T(8,128)}, f32[768,384]{0,1:T(8,128)}, f32[768,384]{0,1:T(8,128)}) fusion(f32[768,384]{0,1:T(8,128)} %copy.108, bf16[768,384]{0,1:T(8,128)(2,1)} %copy.107, f32[768,384]{0,1:T(8,128)} %copy.111, bf16[768,384]{0,1:T(8,128)(2,1)} %copy.110, bf16[2048,384]{1,0:T(8,128)(2,1)} %all-gather.17.cloned.1.call-done, ...), kind=kOutput, calls=%fused_computation.42 | convolution fusion | flops 1211793408 | bytes 12976128 | tf_op jit(solution)/shard_map/dot_general | solution.py:56
  396.9 1.6 copy.112
  398.6 1.2 copy-done.4
  401.3 1.2 mul.213
  402.5 2.9 copy.115
  405.4 3.5 multiply_convert_fusion
  408.9 2.2 copy.120
  413.2 133.7 %reduce-scatter.4.cloned.1.call-done = f32[192,256]{1,0:T(8,128)} async-done(((f32[6144,256]{1,0:T(8,128)}), f32[192,256]{1,0:T(8,128)}) %reduce-scatter.4.cloned.1.call-update) | async-done | bytes 196624
  (50 shorter events, 10.8 us)
Async XLA Ops:
  7.2 85.7 %all-gather.11.cloned.1.call-start = ((), (), s32[]{:S(2)}) async-start(), calls=%async_computation.5 | async-start | bytes 3244032 | tf_op jit(solution)/shard_map/all_gather | solution.py:76
  7.9 119.3 %all-gather.13.cloned.1.call-start = ((), (), s32[]{:S(2)}) async-start(), calls=%async_computation.6 | async-start | bytes 5308416 | tf_op jit(solution)/shard_map/all_gather | solution.py:84
  8.7 201.6 %all-gather.7.cloned.1.call-start = ((), (), s32[]{:S(2)}) async-start(), calls=%async_computation.3 | async-start | bytes 3244032 | tf_op jit(solution)/shard_map/all_gather | solution.py:77
  9.4 235.0 %all-gather.9.cloned.1.call-start = ((), (), s32[]{:S(2)}) async-start(), calls=%async_computation.4 | async-start | bytes 5308416 | tf_op jit(solution)/shard_map/all_gather | solution.py:85
  10.0 350.0 %all-gather.15.cloned.1.call-start = ((), (), s32[]{:S(2)}) async-start(), calls=%async_computation.7 | async-start | bytes 1769472 | tf_op jit(solution)/shard_map/all_gather | solution.py:101
  250.3 140.2 %all-gather.17.cloned.1.call-start = ((), (), s32[]{:S(2)}) async-start(), calls=%async_computation.8 | async-start | bytes 1769472 | tf_op jit(solution)/shard_map/all_gather | solution.py:102
  250.9 296.1 %reduce-scatter.4.cloned.1.call-start = ((), (), s32[]{:S(2)}) async-start(), calls=%async_computation.9 | async-start | bytes 6488064
  264.5 1.9 copy-start
  316.1 41.0 %all-to-all-start.1 = ((bf16[256,8,768]{0,2,1:T(8,128)(2,1)}), bf16[256,8,768]{0,2,1:T(8,128)(2,1)S(1)}, u32[]{:S(2)}, u32[]{:S(2)}) async-start(bf16[256,8,768]{0,2,1:T(8,128)(2,1)} %bitcast.39), calls=%async_computation.1 | async-start | bytes 6291456 | tf_op jit(solution)/shard_map/all_to_all | solution.py:81
  320.2 4.3 copy-start.8
  325.5 2.7 copy-start.9
  332.0 4.3 copy-start.10
  337.4 2.7 copy-start.11
  370.4 1.6 copy-start.5
  384.0 6.5 %copy-start.1 = (bf16[8,256,768]{2,1,0:T(8,128)(2,1)S(1)}, bf16[8,256,768]{2,1,0:T(8,128)(2,1)}, u32[]{:S(2)}) copy-start(bf16[8,256,768]{2,1,0:T(8,128)(2,1)} %copy.109) | copy-start | bytes 9437188
  398.5 1.3 copy-start.4
  402.5 2.9 copy-start.2
  402.5 2.9 copy-start.3
  408.9 2.2 copy-start.7
  408.9 3.3 copy-start.6
Sparse Core Ops, SparseCore 0:
  10.6 82.2 all-gather.10
  94.7 32.4 all-gather.12
  129.8 80.3 all-gather.6
  211.9 32.4 all-gather.8
  250.4 27.9 all-gather.14
  280.1 34.5 all-gather.16
  318.7 228.2 reduce-scatter.3
where the time goes:
time: 557 us; the launch traced here: 556 us
  waiting for transfers between devices  370 us (66%)
  local copies, waits for them, and re-layouts  75.1 us (13%)
  blocking collectives  49.7 us (9%)
  matrix products  31.3 us (6%)
  between operations  14.2 us (3%)
  other arithmetic  11.2 us (2%)
    unnamed x8, waiting for transfers between devices  137 us
    all_gather x1, waiting for transfers between devices, local(): lax.all_gather(tokens, 'col', axis=1, tiled=True)  82.9 us
    all_gather x1, waiting for transfers between devices, local(): lax.all_gather(cotangent, 'col', axis=1, tiled=True)  77.2 us
    all_to_all x1, blocking collectives, local(): lax.all_to_all(token_rows, 'row', split_axis=1, concat_axis=0, tiled=True)  49.7 us
    unnamed x39, local copies, waits for them, and re-layouts  35.3 us
    all_gather x1, waiting for transfers between devices, local(): lax.all_gather(w_expand, 'row', axis=0, tiled=True)  34.3 us
    all_gather x1, waiting for transfers between devices, local(): lax.all_gather(w_reduce, 'row', axis=0, tiled=True)  34.2 us
    mul x16, local copies, waits for them, and re-layouts, spread_scale(): return (shaped * scale[:, None, :]).reshape(values.shape)  26.2 us
  transfers between devices with their start and end apart: 8, of which 6 were waited for; matrix products, arithmetic and copies ran while one was open for 19% of the time, Pallas kernels for 0%

commit v1 on v0

--- a/solution.py
+++ b/solution.py
@@ -74,7 +74,9 @@
 ):
     token_rows, cot_rows = (
         lax.all_gather(tokens, "col", axis=1, tiled=True),
-        lax.all_gather(cotangent, "col", axis=1, tiled=True),
+        jnp.concatenate(
+            lax.all_to_all(jnp.stack([cotangent] * lax.axis_size("col")), "col", 0, 0), axis=1
+        ),
     )
     input_whole, cot_whole = (
         lax.all_to_all(token_rows, "row", split_axis=1, concat_axis=0, tiled=True),

time: 557 us -> 503 us (0.903)
  waiting for transfers between devices: 370 us -> 302 us
  starting transfers between devices: 4.3 us -> 15.7 us
    all_gather x1 -> x0, waiting for transfers between devices: 77.2 us -> none  [local(): lax.all_gather(cotangent, 'col', axis=1, tiled=True)]
    all_to_all x0 -> x1, starting transfers between devices: none -> 11.4 us  [local(): lax.all_to_all(jnp.stack([cotangent] * lax.axis_size('col')), 'col', 0, 0)]
    all_gather x1, waiting for transfers between devices: 82.9 us -> 92.6 us  [local(): lax.all_gather(tokens, 'col', axis=1, tiled=True)]
    unnamed x8 -> x7, waiting for transfers between devices: 137 us -> 136 us
    unnamed x39 -> x41, local copies, waits for them, and re-layouts: 35.3 us -> 35.3 us
  transfers between devices with their start and end apart: 8 -> 8, of which waited for: 6 -> 5; matrix products, arithmetic and copies ran while one was open for 19% -> 22% of each run, Pallas kernels for 0% -> 0%
where the time goes in v1:
time: 503 us; the launch traced here: 502 us
  waiting for transfers between devices  302 us (60%)
  local copies, waits for them, and re-layouts  77.1 us (15%)
  blocking collectives  49.7 us (10%)
  matrix products  31.3 us (6%)
  starting transfers between devices  15.7 us (3%)
  between operations  14.2 us (3%)
  other arithmetic  11.2 us (2%)
    unnamed x7, waiting for transfers between devices  136 us
    all_gather x1, waiting for transfers between devices, local(): lax.all_gather(tokens, 'col', axis=1, tiled=True)  92.6 us
    all_to_all x1, blocking collectives, local(): lax.all_to_all(token_rows, 'row', split_axis=1, concat_axis=0, tiled=True)  49.7 us
    all_gather x1, waiting for transfers between devices, local(): lax.all_gather(w_expand, 'row', axis=0, tiled=True)  36.6 us
    unnamed x41, local copies, waits for them, and re-layouts  35.3 us
    all_gather x1, waiting for transfers between devices, local(): lax.all_gather(w_reduce, 'row', axis=0, tiled=True)  32.8 us
    mul x16, local copies, waits for them, and re-layouts, spread_scale(): return (shaped * scale[:, None, :]).reshape(values.shape)  26.2 us
    dot_general x2, matrix products, contract_first(): lax.dot_general(left, right, (((0,), (0,)), ((), ())), preferred_element_...  12.6 us
  transfers between devices with their start and end apart: 8, of which 5 were waited for; matrix products, arithmetic and copies ran while one was open for 22% of the time, Pallas kernels for 0%

profile of v1, /device:TPU:8, one launch (start us, length us, event | category | flops | bytes accessed | tf_op | source)
XLA Modules:
  0.0 501.6 jit_solution(6521275776533425224)
XLA Ops:
  9.4 2.0 stack.2
  11.4 11.4 %all-to-all-start = ((bf16[32,256,192]{1,2,0:T(8,128)(2,1)}), bf16[32,256,192]{1,2,0:T(8,128)(2,1)}, u32[]{:S(2)}, u32[]{:S(2)}) async-start(bf16[32,256,192]{1,2,0:T(8,128)(2,1)} %stack.2), calls=%async_computation | async-start | bytes 6291456 | tf_op jit(solution)/shard_map/all_to_all | solution.py:78
  22.9 92.6 %all-gather.8.cloned.1.call-done = bf16[256,6144]{0,1:T(8,128)(2,1)} async-done(((bf16[256,192]{0,1:T(8,128)(2,1)}), bf16[256,6144]{0,1:T(8,128)(2,1)}) %all-gather.8.cloned.1.call-update) | async-done | bytes 3145744 | tf_op jit(solution)/shard_map/all_gather | solution.py:76
  115.6 36.6 %all-gather.10.cloned.1.call-done = bf16[6144,384]{1,0:T(8,128)(2,1)} async-done(((bf16[768,384]{1,0:T(8,128)(2,1)}), bf16[6144,384]{1,0:T(8,128)(2,1)}) %all-gather.10.cloned.1.call-update) | async-done | bytes 4718608 | tf_op jit(solution)/shard_map/all_gather | solution.py:86
  152.1 5.8 %multiply_convert_fusion.4 = (bf16[256,384]{1,0:T(8,128)(2,1)}, f32[256,384]{1,0:T(8,128)S(1)}) fusion(bf16[256,6144]{0,1:T(8,128)(2,1)} %all-gather.8.cloned.1.call-done, bf16[6144,384]{1,0:T(8,128)(2,1)} %all-gather.10.cloned.1.call-done), kind=kOutput, calls=%fused_computation.30 | convolution fusion | flops 1208451072 | bytes 8454144 | tf_op jit(solution)/shard_map/dot_general | solution.py:89
  158.0 32.8 %all-gather.6.cloned.1.call-done = bf16[6144,384]{1,0:T(8,128)(2,1)} async-done(((bf16[768,384]{1,0:T(8,128)(2,1)}), bf16[6144,384]{1,0:T(8,128)(2,1)}) %all-gather.6.cloned.1.call-update) | async-done | bytes 4718608 | tf_op jit(solution)/shard_map/all_gather | solution.py:87
  190.8 5.9 %fusion.8 = bf16[256,384]{1,0:T(8,128)(2,1)} fusion(bf16[256,6144]{0,1:T(8,128)(2,1)} %bitcast.1, bf16[6144,384]{1,0:T(8,128)(2,1)} %all-gather.6.cloned.1.call-done, f32[256,384]{1,0:T(8,128)S(1)} %get-tuple-element.82), kind=kOutput, calls=%fused_computation.24 | convolution fusion | flops 1208942592 | bytes 8454144 | tf_op jit(solution)/shard_map/dot_general | solution.py:90
  197.3 7.0 %convolution_bitcast_fusion = f32[6144,256]{0,1:T(8,128)} fusion(bf16[256,384]{1,0:T(8,128)(2,1)} %fusion.8, bf16[6144,384]{1,0:T(8,128)(2,1)} %all-gather.10.cloned.1.call-done), kind=kOutput, calls=%fused_computation | convolution fusion | flops 1207959552 | bytes 11206656 | tf_op jit(solution)/shard_map/dot_general | solution.py:95
  204.3 6.6 %copy.125 = f32[6144,256]{1,0:T(8,128)} copy(f32[6144,256]{0,1:T(8,128)} %convolution_bitcast_fusion) | data formatting | bytes 12582912
  210.9 1.9 copy-done
  212.8 49.7 %all_to_all.43 = bf16[256,8,768]{0,2,1:T(8,128)(2,1)} all-to-all(bf16[256,8,768]{0,2,1:T(8,128)(2,1)S(1)} %bitcast.42), channel_id=1, replica_groups=mesh['row'=8,'col'=32] {'row'}, dimensions={1} | all-to-all | bytes 6291456 | tf_op jit(solution)/shard_map/all_to_all | solution.py:82
  262.5 4.0 all-to-all-start.2
  266.6 2.1 copy.98
  268.7 2.1 copy.108
  271.9 2.7 copy.100
  275.7 2.7 copy.103
  278.4 2.1 copy.102
  280.5 2.1 copy.99
  282.7 1.1 mul.196
  283.8 2.7 copy.110
  286.4 1.1 mul.202
  287.6 2.7 copy.113
  290.2 2.1 copy.109
  292.4 2.1 copy.112
  294.5 4.7 copy.101
  299.2 4.3 all-to-all-done.2
  303.5 2.9 copy.111
  306.4 6.3 %fusion.18 = (f32[768,384]{0,1:T(8,128)}, f32[768,384]{0,1:T(8,128)S(1)}, f32[768,384]{0,1:T(8,128)S(1)}, f32[768,384]{0,1:T(8,128)S(1)}) fusion(f32[768,384]{0,1:T(8,128)} %copy.100, bf16[768,384]{0,1:T(8,128)(2,1)} %copy.99, f32[768,384]{0,1:T(8,128)} %copy.103, bf16[768,384]{0,1:T(8,128)(2,1)} %copy.102, ...), kind=kOutput, calls=%fused_computation.44 | convolution fusion | flops 1211793408 | bytes 12976128 | tf_op jit(solution)/shard_map/dot_general | solution.py:56
  312.7 2.7 copy.104
  315.3 1.4 copy.106
  316.8 1.4 reduce_max.36
  319.0 1.3 broadcast_divide_fusion.2
  320.3 1.1 mul.190
  321.4 1.6 copy.105
  323.1 1.1 mul.193
  324.2 2.7 copy.107
  326.9 3.5 multiply_convert_fusion.2
  330.4 2.3 copy.119
  332.6 2.1 copy.120
  334.8 2.1 copy.121
  336.9 6.4 %fusion.15 = (f32[768,384]{0,1:T(8,128)}, f32[768,384]{0,1:T(8,128)}, f32[768,384]{0,1:T(8,128)}, f32[768,384]{0,1:T(8,128)}) fusion(f32[768,384]{0,1:T(8,128)} %copy.110, bf16[768,384]{0,1:T(8,128)(2,1)} %copy.109, f32[768,384]{0,1:T(8,128)} %copy.113, bf16[768,384]{0,1:T(8,128)(2,1)} %copy.112, bf16[2048,384]{1,0:T(8,128)(2,1)} %all-gather.14.cloned.1.call-done, ...), kind=kOutput, calls=%fused_computation.42 | convolution fusion | flops 1211793408 | bytes 12976128 | tf_op jit(solution)/shard_map/dot_general | solution.py:56
  343.3 1.6 copy.114
  345.0 1.2 copy-done.4
  347.7 1.2 mul.213
  348.9 2.9 copy.117
  351.8 3.5 multiply_convert_fusion
  355.3 2.2 copy.122
  359.6 133.4 %reduce-scatter.4.cloned.1.call-done = f32[192,256]{1,0:T(8,128)} async-done(((f32[6144,256]{1,0:T(8,128)}), f32[192,256]{1,0:T(8,128)}) %reduce-scatter.4.cloned.1.call-update) | async-done | bytes 196624
  (52 shorter events, 11.4 us)
Async XLA Ops:
  7.2 2.2 copy-start.8
  7.2 108.4 %all-gather.8.cloned.1.call-start = ((), (), s32[]{:S(2)}) async-start(), calls=%async_computation.5 | async-start | bytes 3244032 | tf_op jit(solution)/shard_map/all_gather | solution.py:76
  7.9 144.2 %all-gather.10.cloned.1.call-start = ((), (), s32[]{:S(2)}) async-start(), calls=%async_computation.6 | async-start | bytes 5308416 | tf_op jit(solution)/shard_map/all_gather | solution.py:86
  8.7 182.2 %all-gather.6.cloned.1.call-start = ((), (), s32[]{:S(2)}) async-start(), calls=%async_computation.4 | async-start | bytes 5308416 | tf_op jit(solution)/shard_map/all_gather | solution.py:87
  11.4 146.6 %all-to-all-start = ((bf16[32,256,192]{1,2,0:T(8,128)(2,1)}), bf16[32,256,192]{1,2,0:T(8,128)(2,1)}, u32[]{:S(2)}, u32[]{:S(2)}) async-start(bf16[32,256,192]{1,2,0:T(8,128)(2,1)} %stack.2), calls=%async_computation | async-start | bytes 6291456 | tf_op jit(solution)/shard_map/all_to_all | solution.py:78
  22.9 283.5 %all-gather.12.cloned.1.call-start = ((), (), s32[]{:S(2)}) async-start(), calls=%async_computation.7 | async-start | bytes 1769472 | tf_op jit(solution)/shard_map/all_gather | solution.py:103
  196.7 140.2 %all-gather.14.cloned.1.call-start = ((), (), s32[]{:S(2)}) async-start(), calls=%async_computation.8 | async-start | bytes 1769472 | tf_op jit(solution)/shard_map/all_gather | solution.py:104
  197.3 295.7 %reduce-scatter.4.cloned.1.call-start = ((), (), s32[]{:S(2)}) async-start(), calls=%async_computation.9 | async-start | bytes 6488064
  210.9 1.9 copy-start
  262.5 41.0 %all-to-all-start.2 = ((bf16[256,8,768]{0,2,1:T(8,128)(2,1)}), bf16[256,8,768]{0,2,1:T(8,128)(2,1)S(1)}, u32[]{:S(2)}, u32[]{:S(2)}) async-start(bf16[256,8,768]{0,2,1:T(8,128)(2,1)} %bitcast.15), calls=%async_computation.2 | async-start | bytes 6291456 | tf_op jit(solution)/shard_map/all_to_all | solution.py:83
  266.6 4.3 copy-start.9
  271.9 2.7 copy-start.10
  278.4 4.3 copy-start.11
  283.8 2.7 copy-start.12
  316.7 1.6 copy-start.5
  330.4 6.5 %copy-start.1 = (bf16[8,256,768]{2,1,0:T(8,128)(2,1)S(1)}, bf16[8,256,768]{2,1,0:T(8,128)(2,1)}, u32[]{:S(2)}) copy-start(bf16[8,256,768]{2,1,0:T(8,128)(2,1)} %copy.111) | copy-start | bytes 9437188
  344.9 1.3 copy-start.4
  348.9 2.9 copy-start.2
  348.9 2.9 copy-start.3
  355.3 2.2 copy-start.7
  355.3 3.3 copy-start.6
Sparse Core Ops, SparseCore 0:
  10.6 104.9 all-gather.7
  117.4 34.7 all-gather.9
  154.0 36.8 all-gather.5
  196.8 27.9 all-gather.11
  226.5 34.5 all-gather.13
  264.9 228.0 reduce-scatter.3
